TPU v7x, 128 devices: a whole 4x4x4 slice. The times are simulated.
128 devices in a mesh: tm: 16 (over y_hi, z, core), sta: 8 (over y_lo, x).
Axes of the slice: x: 4, y: 4 (y_hi: 2, y_lo: 2; y = y_hi * 2 + y_lo), z: 4, core: 2. Of those that a mesh axis runs over, the one named last changes fastest.
Arguments:
- waveforms: bfloat16 [240, 8192], P('sta', 'tm'), may hold values from -6 to 6
- templates: bfloat16 [32, 64, 240, 100], P('tm', None, 'sta'), may hold values from -6 to 6
- available: int32 [32, 64, 240], P('tm', None, 'sta'), may hold values 0 or 1
- moveout: int32 [32, 64, 240], P('tm', None, 'sta'), may hold values from 0 to 63
- bank_blocks: int32 [2], replicated, may hold values from 0 to 31
Outputs:
- detect_sum: float32 [128, 8192], P('sta', 'tm')
Inputs may be any that keep to these rules, and one draw needn't show every extreme that they name: `bank_blocks`: block b is stored at index b // 2 of tm.
All inputs are finite; a program needn't handle non-finite values. No bound on the sum of `available` on one device may be relied on, other than what follows from the above.
Results may differ from a plain program's by a relative error of at most 0.0029.
Values may be sent and summed in bfloat16 or wider, within the bound.
A program may use at most 128 MiB of HBM per device.

v0:
```python
import jax
import jax.numpy as jnp
from jax import lax
from jax.sharding import PartitionSpec as P

MOVE = 64


epsilon = 1e-06
block_span = 512


def shifted(block, axis, distance):
    devices = range(lax.axis_size(axis))
    route = [(i - distance, i) for i in devices if i - distance in devices]
    return lax.ppermute(block, axis, route)


def spread_2(array, axis, root):
    mine = lax.axis_index(axis) == root
    return lax.psum(jnp.where(mine, array, jnp.zeros_like(array)), axis)


def normalize_bank(bank):
    values = bank.astype(jnp.float32)
    center = jnp.mean(values, axis=-1, keepdims=True)
    deviate = values - center
    spread = jnp.sqrt(jnp.mean(deviate * deviate, axis=-1, keepdims=True) + epsilon)
    return (deviate / (spread * bank.shape[-1])).astype(jnp.bfloat16)


def window_sigma(padded, length, tlen):
    first_sum = jnp.zeros((padded.shape[0], length), jnp.float32)
    second_sum = jnp.zeros((padded.shape[0], length), jnp.float32)
    for lag in range(tlen):
        piece = padded[:, lag : lag + length].astype(jnp.float32)
        first_sum = first_sum + piece
        second_sum = second_sum + piece * piece
    mean_value = first_sum / tlen
    return jnp.sqrt(second_sum / tlen - mean_value * mean_value + epsilon)


def shards(waveforms, templates, available, moveout, bank_blocks):
    channels_dev = waveforms.shape[0]
    samples = waveforms.shape[1]
    blocks_dev = templates.shape[0]
    events = templates.shape[1]
    tlen = templates.shape[3]
    rim_span = MOVE + tlen - 1
    rim_cells = shifted(waveforms[:, :rim_span], "tm", -1)
    extended = jnp.concatenate([waveforms, rim_cells], axis=1)
    sigma = window_sigma(extended, samples + MOVE, tlen)
    owners = bank_blocks // blocks_dev
    slots = bank_blocks % blocks_dev
    bank_list = []
    flag_list = []
    for which in range(2):
        slot_now = slots[which]
        template_portion = lax.dynamic_index_in_dim(templates, slot_now, 0, keepdims=False)
        flag_piece = jnp.stack(
            [
                lax.dynamic_index_in_dim(available, slot_now, 0, keepdims=False),
                lax.dynamic_index_in_dim(moveout, slot_now, 0, keepdims=False),
            ]
        ).astype(jnp.bfloat16)
        template_portion, flag_piece = (template_portion, flag_piece)
        got_bank, got_flags = (
            spread_2(template_portion, "tm", owners[which]),
            spread_2(flag_piece, "tm", owners[which]),
        )
        bank_list.append(got_bank)
        flag_list.append(got_flags.astype(jnp.float32))
    bank_all = jnp.stack(bank_list)
    flag_all = jnp.stack(flag_list)
    unit_norm_templates = normalize_bank(bank_all.reshape(2 * events, channels_dev, tlen))
    weights = flag_all[:, 0].reshape(2 * events, channels_dev)
    shifts = flag_all[:, 1].reshape(2 * events, channels_dev).astype(jnp.int32)
    offsets = jnp.arange(MOVE, dtype=jnp.int32)
    coefficients = jnp.where(shifts[:, :, None] == offsets[None, None, :], weights[:, :, None], 0.0)
    window_width = block_span + MOVE
    own_rows = 2 * events // lax.axis_size("sta")

    def one_window(block):
        reference_sample = block * block_span
        stacked_correlation = jnp.stack(
            [extended[:, lag : lag + window_width] for lag in range(tlen)], axis=1
        )
        correlation_values = jnp.einsum(
            "ofn,fnw->ofw",
            unit_norm_templates,
            stacked_correlation,
            preferred_element_type=jnp.float32,
        )
        scaled_traces = (
            correlation_values
            / lax.dynamic_slice_in_dim(sigma, reference_sample, window_width, 1)[None]
        )
        by_offset = jnp.einsum(
            "tcm,tcw->tmw", coefficients, scaled_traces, precision=lax.Precision.HIGHEST
        )
        flat_rows = by_offset.reshape(own_rows * lax.axis_size("sta"), MOVE * window_width)
        flat_rows = jnp.pad(flat_rows, ((0, 0), (0, MOVE)))
        skewed = flat_rows.reshape(own_rows * lax.axis_size("sta"), MOVE, window_width + 1)
        return jnp.sum(skewed[:, :, :block_span], axis=1)

    result = lax.map(one_window, jnp.arange(samples // block_span, dtype=jnp.int32))
    return lax.psum_scatter(
        jnp.transpose(result, (1, 0, 2)).reshape(own_rows * lax.axis_size("sta"), samples),
        "sta",
        scatter_dimension=0,
        tiled=True,
    )


def solution(mesh):
    in_specs = (
        P("sta", "tm"),
        P("tm", None, "sta", None),
        P("tm", None, "sta"),
        P("tm", None, "sta"),
        P(),
    )
    out_specs = P("sta", "tm")
    return jax.shard_map(shards, mesh=mesh, in_specs=in_specs, out_specs=out_specs, check_vma=False)
```

profile of v0, /device:TPU:0, one launch (start us, length us, event | category | flops | bytes accessed | tf_op | source)
XLA Modules:
  0.0 323.1 jit_solution(16816527787224804560)
XLA Ops:
  6.5 0.7 slice.533
  7.3 1.3 collective-permute-start
  14.9 2.3 dynamic-slice_select_fusion.1
  17.2 0.9 dynamic-slice_convert_fusion.2
  18.1 0.9 dynamic-slice_convert_fusion.3
  19.1 72.5 %all-reduce.1 = (bf16[1,2,64,30]{2,0,3,1:T(2,128)(2,1)S(1)}, bf16[1,2,64,30]{2,0,3,1:T(2,128)(2,1)S(1)}) all-reduce(bf16[1,2,64,30]{2,0,3,1:T(2,128)(2,1)S(1)} %copy.3426, bf16[1,2,64,30]{2,0,3,1:T(2,128)(2,1)S(1)} %copy.3425), channel_id=1, replica_groups=mesh['tm'=16,'sta'=8] {'tm'}, use_global_device_ids=true, to_apply=%region_1.2 | all-reduce | flops 7680 | bytes 30720 | tf_op jit(solution)/shard_map/psum | solution.py:21
  91.7 0.8 constant_dynamic-update-slice_fusion.1
  97.3 0.7 copy.3470
  98.0 0.7 copy.3469
  98.7 0.7 copy.3468
  99.4 0.7 copy.3467
  101.5 0.7 copy.3464
  102.2 0.7 copy.3463
  103.5 0.7 copy.3461
  105.6 0.7 copy.3458
  108.3 0.7 copy.3454
  109.0 0.7 copy.3453
  112.1 0.7 copy.3506
  112.8 0.7 copy.3505
  115.5 0.7 copy.3501
  116.2 0.7 copy.3500
  119.6 0.7 copy.3495
  122.4 0.7 copy.3491
  123.3 0.7 copy.3490
  124.7 0.7 copy.3488
  125.4 0.7 copy.3487
  127.5 0.7 copy.3484
  128.9 0.7 copy.3482
  129.6 0.7 copy.3481
  130.2 0.7 copy.3480
  131.0 0.7 copy.3479
  131.7 0.7 copy.3478
  132.3 0.7 copy.3477
  136.4 33.3 %stack.545 = bf16[30,100,576]{2,1,0:T(8,128)(2,1)} concatenate(bf16[30,1,576]{2,1,0:T(2,128)(2,1)S(1)} %copy.3429, bf16[30,1,576]{2,1,0:T(2,128)(2,1)S(1)} %copy.3430, bf16[30,1,576]{2,1,0:T(2,128)(2,1)S(1)} %copy.3431, bf16[30,1,576]{2,1,0:T(2,128)(2,1)S(1)} %copy.3432, bf16[30,1,576]{2,1,0:T(2,128)(2,1)S(1)} %copy.3433, bf16[30,1,576]{2,1,0:T(2,128)(2,1)S(1)} %copy.3434, ...), dimensions={1} | concatenate | bytes 6912000 | tf_op jit(solution)/shard_map/while/body/eval_jaxpr/stack | solution.py:85
  169.8 1.6 fusion.111
  171.4 1.8 fusion.7
  173.2 2.3 multiply_reduce_fusion
  175.6 1.5 maximum_convert_fusion
  177.4 1.4 fusion.3
  179.4 6.3 %divide_bitcast_fusion = f32[128,30,576]{0,2,1:T(8,128)} fusion(f32[30,576]{1,0:T(8,128)S(1)} %fusion.111, bf16[30,100,576]{2,1,0:T(8,128)(2,1)S(1)} %copy-done, bf16[128,30,100]{2,0,1:T(8,128)(2,1)S(1)} %fusion.3), kind=kOutput, calls=%fused_computation.1 | convolution fusion | flops 444579840 | bytes 13140480 | tf_op jit(solution)/shard_map/while/body/eval_jaxpr/ofn,fnw->ofw/dot_general | solution.py:88
  185.7 12.0 %copy.3533 = f32[128,30,576]{2,1,0:T(8,128)} copy(f32[128,30,576]{0,2,1:T(8,128)} %divide_bitcast_fusion) | data formatting | bytes 17694720 | tf_op jit(solution)/shard_map/while/body/eval_jaxpr/div | solution.py:95
  197.7 25.3 %fusion = f32[128,64,576]{2,1,0:T(8,128)} fusion(f32[128,30,576]{2,1,0:T(8,128)} %copy.3533, f32[128,30]{1,0:T(8,128)S(1)} %bitcast.231, s32[128,30]{1,0:T(8,128)S(1)} %bitcast.230), kind=kOutput, calls=%fused_computation.2 | convolution fusion | flops 1699184640 | bytes 27752448 | tf_op jit(solution)/shard_map/while/body/eval_jaxpr/tcm,tcw->tmw/dot_general | solution.py:98
  223.0 22.3 %copy.3534 = f32[128,64,576]{0,2,1:T(8,128)} copy(f32[128,64,576]{2,1,0:T(8,128)} %fusion) | data formatting | bytes 37748736 | tf_op jit(solution)/shard_map/while/body/eval_jaxpr/tcm,tcw->tmw/dot_general | solution.py:98
  245.3 14.5 %pad.5 = f32[128,36928]{0,1:T(8,128)} pad(f32[128,36864]{0,1:T(8,128)} %bitcast.229, f32[]{:T(128)} %constant.78.clone.1), padding=0_0x0_64 | pad | bytes 37781508 | tf_op jit(solution)/shard_map/while/body/eval_jaxpr/jit(_pad)/pad | solution.py:102
  259.8 15.1 %reshape.60 = f32[128,64,577]{0,2,1:T(8,128)} reshape(f32[128,36928]{0,1:T(8,128)} %pad.5) | data formatting | bytes 37814272 | tf_op jit(solution)/shard_map/while/body/eval_jaxpr/reshape | solution.py:103
  274.9 6.6 %slice_reduce_fusion = f32[128,512]{0,1:T(8,128)S(1)} fusion(f32[128,64,577]{0,2,1:T(8,128)} %reshape.60), kind=kLoop, calls=%fused_computation | loop fusion | flops 4128768 | bytes 17039360 | tf_op jit(solution)/shard_map/while/body/eval_jaxpr/reduce_sum | solution.py:104
  281.4 0.8 copy.3539
  282.3 34.0 %reduce-scatter.4.cloned.1.call-done = f32[16,512]{1,0:T(8,128)} async-done(((f32[128,512]{1,0:T(8,128)}), f32[16,512]{1,0:T(8,128)}) %reduce-scatter.4.cloned.1.call-update) | async-done | bytes 32784 | tf_op jit(solution)/shard_map/reduce_scatter | solution.py:107
  (106 shorter events, 28.1 us)
Async XLA Ops:
  6.5 164.9 %all-reduce.5.cloned.1.call-start = ((), (), s32[]{:S(2)}) async-start(), calls=%async_computation.2 | async-start | bytes 1966080 | tf_op jit(solution)/shard_map/psum | solution.py:21
  7.3 85.4 %collective-permute-start = (bf16[30,163]{1,0:T(8,128)(2,1)S(1)}, bf16[30,163]{1,0:T(8,128)(2,1)S(1)}, u32[]{:S(2)}, u32[]{:S(2)}) collective-permute-start(bf16[30,163]{1,0:T(8,128)(2,1)S(1)} %slice.533), channel_id=1, source_target_pairs={{8,0},{16,8},{24,16},{32,24},{40,32},{48,40},{56,48},{64,56},{72,6... | collective-permute-start | bytes 29348 | tf_op jit(solution)/shard_map/ppermute | solution.py:16
  17.1 299.2 %reduce-scatter.4.cloned.1.call-start = ((), (), s32[]{:S(2)}) async-start(), calls=%async_computation.1 | async-start | bytes 294912 | tf_op jit(solution)/shard_map/reduce_scatter | solution.py:107
  177.3 2.1 copy-start
Sparse Core Ops, SparseCore 0:
  17.3 143.9 all-reduce.4
  282.4 33.8 reduce-scatter.3
where the time goes:
time: 326 us; the launch traced here: 323 us
  local copies, waits for them, and re-layouts  145 us (44%)
  blocking collectives  72.5 us (22%)
  waiting for transfers between devices  34.1 us (10%)
  matrix products  31.5 us (10%)
  other arithmetic  20.1 us (6%)
  between operations  18.9 us (6%)
    another operation x107, local copies, waits for them, and re-layouts, one_window(): jnp.stack([extended[:, lag:lag + window_width] for lag in range(tlen)], a...  76.6 us
    psum x1, blocking collectives, spread_2(): return lax.psum(jnp.where(mine, array, jnp.zeros_like(array)), axis)  72.5 us
    reduce_scatter x1, waiting for transfers between devices, shards(): lax.psum_scatter(jnp.transpose(result, (1, 0, 2)).reshape(own_rows * lax....  34 us
    dot_general x1, matrix products, one_window(): jnp.einsum('tcm,tcw->tmw', coefficients, scaled_traces, precision=lax.Pre...  25.3 us
    dot_general x1, local copies, waits for them, and re-layouts, one_window(): jnp.einsum('tcm,tcw->tmw', coefficients, scaled_traces, precision=lax.Pre...  22.3 us
    reshape x1, local copies, waits for them, and re-layouts, one_window(): flat_rows.reshape(own_rows * lax.axis_size('sta'), MOVE, window_width + 1)  15.1 us
    pad x1, local copies, waits for them, and re-layouts, one_window(): flat_rows = jnp.pad(flat_rows, ((0, 0), (0, MOVE)))  14.5 us
    div x1, local copies, waits for them, and re-layouts, one_window(): correlation_values / lax.dynamic_slice_in_dim(sigma, reference_sample, wi...  12 us
  transfers between devices with their start and end apart: 3, of which 1 were waited for; matrix products, arithmetic and copies ran while one was open for 26% of the time, Pallas kernels for 0%

commit v1 on v0

v1 whole, which is shorter than its diff:
```python
import jax
import jax.numpy as jnp
from jax import lax
from jax.experimental import pallas as pl
from jax.experimental.pallas import tpu as pltpu
from jax.sharding import PartitionSpec as P

TLEN = 100
MOVE = 64
EPS = 1e-06
SEG = 512
EXT = 768
CORR = 640
CH = 30
ROWS = 32
LANES = 128
HROWS = 112
MESH = pl.DeviceIdType.MESH
VMEM = pltpu.VMEM
MIB = 1 << 20


def place():
    tm = lax.axis_index("tm")
    return tm // 8, (tm // 2) % 4, tm % 2


def at_tm(y, z, h):
    return {"tm": y * 8 + z * 2 + h}


def remote(src, dst, send, recv, device):
    return pltpu.make_async_remote_copy(
        src_ref=src, dst_ref=dst, send_sem=send, recv_sem=recv, device_id=device, device_id_type=MESH
    )


def exchange_kernel(
    blocks, bank, wave, got_bank, got_wave, got_halo, cores, cand, pieces,
    local_sem, wave_send, wave_recv, halo_send, halo_recv, core_send, core_recv,
    piece_send, piece_recv, gather_send, gather_recv,
):
    y, z, h = place()
    barrier = pltpu.get_barrier_semaphore()
    tm = lax.axis_index("tm")
    own = pltpu.make_async_copy(bank.at[:, pl.ds(32 * h, 32)], cores.at[h], local_sem.at[0])
    own.start()
    own_wave = pltpu.make_async_copy(wave, got_wave.at[y, h], local_sem.at[1])
    own_wave.start()
    for d in range(1, 16):
        pl.semaphore_signal(barrier, inc=1, device_id={"tm": (tm + d) % 16}, device_id_type=MESH)
    pl.semaphore_wait(barrier, 15)

    to_core = remote(
        bank.at[:, pl.ds(32 * (1 - h), 32)], cores.at[h], core_send, core_recv, at_tm(y, z, 1 - h)
    )
    to_core.start()
    waves = []
    for dy, dh in ((0, 1), (1, 0), (1, 1)):
        i = dy * 2 + dh - 1
        copy = remote(
            wave, got_wave.at[y, h], wave_send.at[i], wave_recv.at[i],
            at_tm((y + dy) % 2, z, (h + dh) % 2),
        )
        copy.start()
        waves.append(copy)

    run = jnp.where(z > 0, y, 1 - y)

    def halo_copy(k):
        return remote(
            wave.at[:, pl.ds(0, 256)], got_halo.at[run], halo_send.at[k], halo_recv.at[run],
            at_tm(k // 2, (z + 3) % 4, k % 2),
        )

    @pl.when(h == 0)
    def _():
        for k in range(4):
            halo_copy(k).start()

    own.wait()
    to_core.wait()
    for q in range(2):
        b = blocks[q]
        cand[q] = cores[(b // 2) % 2, b % 2]

    sends = []
    for d in range(1, 8):
        y2, z2 = (y + d // 4) % 2, (z + d) % 4
        copy = remote(
            cand.at[y2, pl.ds(8 * z2, 8)], pieces.at[y, z], piece_send.at[d - 1], piece_recv.at[d - 1],
            at_tm(y2, z2, h),
        )
        copy.start()
        sends.append(copy)
    pieces[y, z] = cand[y, pl.ds(8 * z, 8)]
    for copy in sends:
        copy.wait()
    owner = blocks[y] // 2
    got_bank[z] = pieces[owner // 8, (owner // 2) % 4]
    gathers = []
    for d in range(1, 4):
        copy = remote(
            got_bank.at[z], got_bank.at[z], gather_send.at[d - 1], gather_recv.at[d - 1],
            at_tm(y, (z + d) % 4, h),
        )
        copy.start()
        gathers.append(copy)
    own_wave.wait()
    for copy in waves:
        copy.wait()
    for r in range(2):
        remote(
            wave.at[:, pl.ds(0, 256)], got_halo.at[r], halo_send.at[0], halo_recv.at[r], at_tm(0, (z + 1) % 4, 0)
        ).wait_recv()

    @pl.when(h == 0)
    def _():
        for k in range(4):
            halo_copy(k).wait_send()

    for copy in gathers:
        copy.wait()


def left(x, n):
    return pltpu.roll(x, x.shape[1] - n, 1)


def window_sum(x):
    two = x + left(x, 1)
    four = two + left(two, 2)
    eight = four + left(four, 4)
    sixteen = eight + left(eight, 8)
    half = sixteen + left(sixteen, 16)
    full = half + left(half, 32)
    return full + left(half, 64) + left(four, 96)


def correlate_kernel(bank, wave, halo, out, rows32, unit, index, ext, scale, hankel):
    y, z, h = place()
    lane = lax.broadcasted_iota(jnp.int32, (ROWS, LANES), 1)
    for s in range(4):
        run, core = s // 2, s % 2
        ext[s, 0:CH, 0:SEG] = wave[run, core].astype(jnp.float32)
        if core == 0:
            tail = wave[run, 1, :, 0:256].astype(jnp.float32)
        else:
            tail = halo[run].astype(jnp.float32)
            if run == 1:
                tail = jnp.where(z == 3, jnp.zeros_like(tail), tail)
        ext[s, 0:CH, SEG:EXT] = tail

    @pl.loop(0, 4)
    def _(s):
        x = ext[s]
        first = window_sum(x)[:, :CORR] * (1.0 / TLEN)
        second = window_sum(x * x)[:, :CORR] * (1.0 / TLEN)
        scale[s] = lax.rsqrt(second - first * first + EPS)

        @pl.loop(0, CH)
        def _(c):
            row = ext[s, pl.ds(c, 1), :]
            wide = jnp.broadcast_to(row, (HROWS, EXT))
            turned = pltpu.roll(wide, EXT - (HROWS - 1), 1, stride=1, stride_axis=0)
            hankel[s, c, 0:HROWS, :] = turned[:, :CORR].astype(jnp.bfloat16)
            hankel[s, c, HROWS:, :] = jnp.zeros((LANES - HROWS, CORR), jnp.bfloat16)

    lane8 = lax.broadcasted_iota(jnp.int32, (ROWS, LANES), 1)
    live = lane8 < TLEN

    @pl.loop(0, 32)
    def _(t):
        v = bank[t].astype(jnp.float32)
        v = jnp.where(live, v, 0.0)
        mean = jnp.sum(v, axis=1, keepdims=True) * (1.0 / TLEN)
        dev = jnp.where(live, v - mean, 0.0)
        spread = jnp.sqrt(jnp.sum(dev * dev, axis=1, keepdims=True) * (1.0 / TLEN) + EPS)
        u = dev / (spread * TLEN)
        sub = lax.broadcasted_iota(jnp.int32, (ROWS, LANES), 0)
        rows32[pl.ds(32 * t, 32), :] = jnp.where(sub < CH, u, v)

    avail = rows32[pl.ds(CH, 32, stride=32), :]
    shift = rows32[pl.ds(CH + 1, 32, stride=32), :]
    flip = (HROWS - 1 - lane) & (LANES - 1)
    for c in range(CH):
        u = rows32[pl.ds(c, 32, stride=32), :] * avail[:, c : c + 1]
        unit[c] = jnp.take_along_axis(u, flip, axis=1).astype(jnp.bfloat16)
        index[c] = lane + jnp.broadcast_to(shift[:, c : c + 1], (32, LANES)).astype(jnp.int32)

    for s in range(4):
        def channel(c, acc):
            corr = jnp.dot(unit[c], hankel[s, c], preferred_element_type=jnp.float32)
            corr = corr * scale[s, pl.ds(c, 1), :]
            where = index[c]
            inside = where < LANES
            at = where & (LANES - 1)
            turned = [
                jnp.take_along_axis(corr[:, LANES * m : LANES * (m + 1)], at, axis=1) for m in range(5)
            ]
            return tuple(a + jnp.where(inside, turned[m], turned[m + 1]) for m, a in enumerate(acc))

        acc = lax.fori_loop(
            0, CH, channel, tuple(jnp.zeros((32, LANES), jnp.float32) for _ in range(4)), unroll=5
        )
        for m in range(4):
            out[s, :, LANES * m : LANES * (m + 1)] = acc[m]


def reduce_kernel(part, out, got, send, recv):
    y, z, h = place()
    sta = lax.axis_index("sta")
    tm = lax.axis_index("tm")
    from_y, from_h = sta // 4, (sta // 2) % 2
    source_tm = from_y * 8 + z * 2 + from_h
    mine = source_tm == tm
    barrier = pltpu.get_barrier_semaphore()
    for s in range(8):
        @pl.when(jnp.logical_not(jnp.logical_and(mine, sta == s)))
        def _():
            pl.semaphore_signal(
                barrier, inc=1, device_id={"tm": source_tm, "sta": s}, device_id_type=MESH
            )

    @pl.when(mine)
    def _():
        pl.semaphore_wait(barrier, 7)

    @pl.when(jnp.logical_not(mine))
    def _():
        pl.semaphore_wait(barrier, 8)

    def copy(k):
        y2, h2, j = k // 4, (k // 2) % 2, k % 2
        to_tm = y2 * 8 + z * 2 + h2
        to_sta = 4 * y + 2 * h + j
        itself = jnp.logical_and(to_tm == tm, to_sta == sta)
        src = part.at[2 * y2 + h2, pl.ds(16 * j, 16)]
        return itself, src, remote(src, got.at[sta], send.at[k], recv.at[sta], {"tm": to_tm, "sta": to_sta})

    for k in range(8):
        itself, src, away = copy(k)

        @pl.when(jnp.logical_not(itself))
        def _():
            away.start()

        @pl.when(itself)
        def _():
            got[sta] = src[...]

    for k in range(8):
        itself, src, away = copy(k)

        @pl.when(jnp.logical_not(itself))
        def _():
            away.wait_send()

    for s in range(8):
        @pl.when(jnp.logical_not(jnp.logical_and(mine, sta == s)))
        def _():
            remote(
                part.at[0, pl.ds(0, 16)], got.at[s], send.at[0], recv.at[s], {"tm": source_tm, "sta": s}
            ).wait_recv()

    total = got[0]
    for s in range(1, 8):
        total = total + got[s]
    out[...] = total


ANY = pl.BlockSpec(memory_space=pl.ANY)
IN_VMEM = pl.BlockSpec(memory_space=VMEM)
IN_SMEM = pl.BlockSpec(memory_space=pltpu.SMEM)
DMA = pltpu.SemaphoreType.DMA


def shards(waveforms, templates, available, moveout, bank_blocks):
    flags = jnp.stack([available, moveout], axis=2).astype(jnp.bfloat16)
    flags = jnp.pad(flags, ((0, 0), (0, 0), (0, 0), (0, LANES - CH)))
    bank = jnp.concatenate([jnp.pad(templates, ((0, 0), (0, 0), (0, 0), (0, LANES - TLEN))), flags], axis=2)
    bf16, f32 = jnp.bfloat16, jnp.float32
    got_bank, got_wave, got_halo = pl.pallas_call(
        exchange_kernel,
        out_shape=(
            jax.ShapeDtypeStruct((4, 8, ROWS, LANES), bf16),
            jax.ShapeDtypeStruct((2, 2, CH, SEG), bf16),
            jax.ShapeDtypeStruct((2, CH, 256), bf16),
        ),
        in_specs=[IN_SMEM, ANY, ANY],
        out_specs=(IN_VMEM, IN_VMEM, IN_VMEM),
        scratch_shapes=[
            VMEM((2, 2, 32, ROWS, LANES), bf16),
            VMEM((2, 32, ROWS, LANES), bf16),
            VMEM((2, 4, 8, ROWS, LANES), bf16),
            DMA((2,)), DMA((3,)), DMA((3,)), DMA((4,)), DMA((2,)), DMA, DMA,
            DMA((7,)), DMA((7,)), DMA((3,)), DMA((3,)),
        ],
        compiler_params=pltpu.CompilerParams(collective_id=1, has_side_effects=True, vmem_limit_bytes=40 * MIB),
    )(bank_blocks, bank, waveforms)
    part = pl.pallas_call(
        correlate_kernel,
        out_shape=jax.ShapeDtypeStruct((4, 32, SEG), f32),
        in_specs=[IN_VMEM, IN_VMEM, IN_VMEM],
        out_specs=IN_VMEM,
        scratch_shapes=[
            VMEM((32 * ROWS, LANES), f32),
            VMEM((CH, 32, LANES), bf16),
            VMEM((CH, 32, LANES), jnp.int32),
            VMEM((4, ROWS, EXT), f32),
            VMEM((4, ROWS, CORR), f32),
            VMEM((4, CH, LANES, CORR), bf16),
        ],
        compiler_params=pltpu.CompilerParams(vmem_limit_bytes=56 * MIB),
    )(got_bank.reshape(32, ROWS, LANES), got_wave, got_halo)
    return pl.pallas_call(
        reduce_kernel,
        out_shape=jax.ShapeDtypeStruct((16, SEG), f32),
        in_specs=[IN_VMEM],
        out_specs=IN_VMEM,
        scratch_shapes=[VMEM((8, 16, SEG), f32), DMA((8,)), DMA((8,))],
        compiler_params=pltpu.CompilerParams(collective_id=2, has_side_effects=True),
    )(part)


def solution(mesh):
    in_specs = (
        P("sta", "tm"),
        P("tm", None, "sta", None),
        P("tm", None, "sta"),
        P("tm", None, "sta"),
        P(),
    )
    return jax.shard_map(shards, mesh=mesh, in_specs=in_specs, out_specs=P("sta", "tm"), check_vma=False)
```

time: 326 us -> 80.1 us (0.25)
  the two profiles are of different devices: /device:TPU:0 before, /device:TPU:11 now
where the time goes in v1:
time: 80.1 us; the launch traced here: 78.9 us
  Pallas kernels  70.9 us (89%)
  local copies, waits for them, and re-layouts  5.8 us (7%)
  other arithmetic  2.09 us (3%)
    pallas_call x1, Pallas kernels, shards(): pl.pallas_call(correlate_kernel, out_shape=jax.ShapeDtypeStruct((4, 32, S...  36.8 us
    pallas_call x1, Pallas kernels, shards(): pl.pallas_call(exchange_kernel, out_shape=(jax.ShapeDtypeStruct((4, 8, RO...  21.4 us
    pallas_call x1, Pallas kernels, shards(): pl.pallas_call(reduce_kernel, out_shape=jax.ShapeDtypeStruct((16, SEG), f...  12.7 us
    unnamed x12, local copies, waits for them, and re-layouts  5.57 us
    another operation x3, other arithmetic, shards(): flags = jnp.stack([available, moveout], axis=2).astype(jnp.bfloat16)  1.74 us

profile of v1, /device:TPU:11, one launch (start us, length us, event | category | flops | bytes accessed | tf_op | source)
XLA Modules:
  0.0 78.9 jit_solution(11086174906848812006)
XLA Ops:
  0.0 0.8 convert_bitcast_fusion.1
  0.8 0.8 convert_bitcast_fusion
  1.5 0.1 copy.18
  1.7 0.1 copy.17
  1.8 0.2 fusion.4
  2.0 1.9 %copy.16 = bf16[2,64,30,100]{3,2,1,0:T(8,128)(2,1)S(1)} copy(bf16[2,64,30,100]{3,1,2,0:T(8,128)(2,1)} %param.6) | data formatting | bytes 1536000 | tf_op args[1]
  3.8 0.0 copy-start.2
  3.9 0.0 copy-start.4
  3.9 0.3 fusion.1.bank
  4.2 0.4 copy-done.2
  4.6 0.0 copy-done.4
  4.6 21.4 %shard_map.55 = (bf16[4,8,32,128]{3,2,1,0:T(8,128)(2,1)S(1)}, bf16[2,2,30,512]{3,2,1,0:T(8,128)(2,1)S(1)}, bf16[2,30,256]{2,1,0:T(8,128)(2,1)S(1)}) custom-call(s32[2]{0:T(128)S(1)} %copy-done.4, bf16[2,64,32,128]{3,2,1,0:T(8,128)(2,1)S(1)} %fusion.1.bank, bf16[30,512]{1,0:T(8,128)(2,1)S(1)} %copy-done.2), custom_call_target="tpu_custom_call" | custom-call | tf_op jit(solution)/shard_map/pallas_call | solution.py:283
  26.0 0.0 copy-start
  26.0 0.7 copy-done
  26.7 0.0 copy-start.1
  26.7 0.6 copy-done.1
  27.4 0.0 copy-start.3
  27.4 0.6 copy-done.3
  28.0 36.8 %shard_map.56.part = f32[4,32,512]{2,1,0:T(8,128)} custom-call(bf16[32,32,128]{2,1,0:T(8,128)(2,1)} %bitcast.5, bf16[2,2,30,512]{3,2,1,0:T(8,128)(2,1)} %copy-done.1, bf16[2,30,256]{2,1,0:T(8,128)(2,1)} %copy-done.3), custom_call_target="tpu_custom_call" | custom-call | tf_op jit(solution)/shard_map/pallas_call | solution.py:301
  64.8 12.7 %shard_map.57 = f32[16,512]{1,0:T(8,128)} custom-call(f32[4,32,512]{2,1,0:T(8,128)} %shard_map.56.part), custom_call_target="tpu_custom_call" | custom-call | tf_op jit(solution)/shard_map/pallas_call | solution.py:316
  77.5 1.4 %copy.20 = f32[16,512]{1,0:T(8,128)} copy(f32[16,512]{1,0:T(8,128)} %shard_map.57) | data formatting | bytes 65536
Async XLA Ops:
  3.8 0.8 copy-start.2
  3.9 0.8 copy-start.4
  26.0 0.7 copy-start
  26.7 0.6 copy-start.1
  27.4 0.6 copy-start.3

commit v2 on v0

v2 whole, which is shorter than its diff:
```python
import jax
import jax.numpy as jnp
from jax import lax
from jax.experimental import pallas as pl
from jax.experimental.pallas import tpu as pltpu
from jax.sharding import PartitionSpec as P

TLEN = 100
EPS = 1e-06
SEG = 512
EXT = 768
CORR = 640
CH = 30
ROWS = 32
LANES = 128
HROWS = 112
CHUNKS = ((0, 15), (15, 30))
HELD = (17, 15)
MESH = pl.DeviceIdType.MESH
VMEM = pltpu.VMEM
DMA = pltpu.SemaphoreType.DMA
MIB = 1 << 20


def place():
    tm = lax.axis_index("tm")
    return tm // 8, (tm // 2) % 4, tm % 2


def at_tm(y, z, h):
    return {"tm": y * 8 + z * 2 + h}


def remote(src, dst, send, recv, device):
    return pltpu.make_async_remote_copy(
        src_ref=src, dst_ref=dst, send_sem=send, recv_sem=recv, device_id=device, device_id_type=MESH
    )


def left(x, n):
    return pltpu.roll(x, x.shape[1] - n, 1)


def window_sum(x):
    two = x + left(x, 1)
    four = two + left(two, 2)
    eight = four + left(four, 4)
    sixteen = eight + left(eight, 8)
    half = sixteen + left(sixteen, 16)
    full = half + left(half, 32)
    return full + left(half, 64) + left(four, 96)


def kernel(
    blocks, bank, avail, shift, wave, out,
    cores0, cores1, core_flags, cand0, cand1, pieces0, pieces1, got0, got1, got_wave, got_halo,
    ext, scale, hankel, unit, index, part, got_part,
    local_sem, wave_send, wave_recv, halo_send, halo_recv, core_send, core_recv,
    piece_send, piece_recv, gather_send, gather_recv, part_send, part_recv,
):
    y, z, h = place()
    tm = lax.axis_index("tm")
    sta = lax.axis_index("sta")
    flags = (avail, shift)
    cores, cand, pieces, got = (cores0, cores1), (cand0, cand1), (pieces0, pieces1), (got0, got1)
    locals_ = [
        pltpu.make_async_copy(bank.at[:, a:b, pl.ds(32 * h, 32)], cores[i].at[h], local_sem.at[i])
        for i, (a, b) in enumerate(CHUNKS)
    ]
    local_flags = [pltpu.make_async_copy(flags[f], core_flags.at[h, f], local_sem.at[2 + f]) for f in range(2)]
    local_wave = pltpu.make_async_copy(wave, got_wave.at[y, h], local_sem.at[4])
    for copy in locals_ + local_flags + [local_wave]:
        copy.start()

    source_tm = (sta // 4) * 8 + z * 2 + (sta // 2) % 2
    mine = source_tm == tm
    barrier = pltpu.get_barrier_semaphore()
    for d in range(1, 16):
        pl.semaphore_signal(barrier, inc=1, device_id={"tm": (tm + d) % 16}, device_id_type=MESH)
    for s in range(8):
        @pl.when(jnp.logical_not(jnp.logical_and(mine, sta == s)))
        def _():
            pl.semaphore_signal(barrier, inc=1, device_id={"tm": source_tm, "sta": s}, device_id_type=MESH)

    @pl.when(mine)
    def _():
        pl.semaphore_wait(barrier, 22)

    @pl.when(jnp.logical_not(mine))
    def _():
        pl.semaphore_wait(barrier, 23)

    partner = at_tm(y, z, 1 - h)
    to_flags = [
        remote(flags[f], core_flags.at[h, f], core_send.at[2 + f], core_recv.at[2 + f], partner) for f in range(2)
    ]
    to_core = [
        remote(
            bank.at[:, a:b, pl.ds(32 * (1 - h), 32)], cores[i].at[h], core_send.at[i], core_recv.at[i], partner
        )
        for i, (a, b) in enumerate(CHUNKS)
    ]
    for copy in to_flags + to_core:
        copy.start()
    waves = []
    for dy, dh in ((0, 1), (1, 0), (1, 1)):
        i = dy * 2 + dh - 1
        copy = remote(
            wave, got_wave.at[y, h], wave_send.at[i], wave_recv.at[i], at_tm((y + dy) % 2, z, (h + dh) % 2)
        )
        copy.start()
        waves.append(copy)

    run = jnp.where(z > 0, y, 1 - y)

    def halo_copy(k):
        return remote(
            wave.at[:, pl.ds(0, 256)], got_halo.at[run], halo_send.at[k], halo_recv.at[run],
            at_tm(k // 2, (z + 3) % 4, k % 2),
        )

    @pl.when(h == 0)
    def _():
        for k in range(4):
            halo_copy(k).start()

    for copy in local_flags + to_flags:
        copy.wait()
    sends = []
    for i, (a, b) in enumerate(CHUNKS):
        locals_[i].wait()
        to_core[i].wait()
        for q in range(2):
            block = blocks[q]
            core, slot = (block // 2) % 2, block % 2
            for z2 in range(4):
                cand[i][q, z2, 0 : b - a, :, 0:TLEN] = cores[i][core, slot, :, 8 * z2 : 8 * z2 + 8]
            if i == 0:
                for f in range(2):
                    both = core_flags[core, f].astype(jnp.float32)
                    rows = jnp.where(slot == 0, both[:, 0, :], both[:, 1, :]).astype(jnp.bfloat16)
                    for z2 in range(4):
                        top = min(8, CH - 8 * z2)
                        cand[i][q, z2, b - a + f, 0:top, 0:64] = rows[8 * z2 : 8 * z2 + top]
        for d in range(1, 8):
            y2, z2 = (y + d // 4) % 2, (z + d) % 4
            copy = remote(
                cand[i].at[y2, z2], pieces[i].at[y, z], piece_send.at[i, d - 1], piece_recv.at[i, d - 1],
                at_tm(y2, z2, h),
            )
            copy.start()
            sends.append((i, copy))

    local_wave.wait()
    for copy in waves:
        copy.wait()
    for r in range(2):
        remote(
            wave.at[:, pl.ds(0, 256)], got_halo.at[r], halo_send.at[0], halo_recv.at[r], at_tm(0, (z + 1) % 4, 0)
        ).wait_recv()
    for s in range(4):
        run, core = s // 2, s % 2
        ext[s, 0:CH, 0:SEG] = got_wave[run, core].astype(jnp.float32)
        if core == 0:
            tail = got_wave[run, 1, :, 0:256].astype(jnp.float32)
        else:
            tail = got_halo[run].astype(jnp.float32)
            if run == 1:
                tail = jnp.where(z == 3, jnp.zeros_like(tail), tail)
        ext[s, 0:CH, SEG:EXT] = tail

    def lags(s):
        x = ext[s]
        first = window_sum(x)[:, :CORR] * (1.0 / TLEN)
        second = window_sum(x * x)[:, :CORR] * (1.0 / TLEN)
        scale[s] = lax.rsqrt(second - first * first + EPS)

        def one(c, carry):
            wide = jnp.broadcast_to(ext[s, pl.ds(c, 1), :], (HROWS, EXT))
            turned = pltpu.roll(wide, EXT - (HROWS - 1), 1, stride=1, stride_axis=0)
            hankel[s, c, 0:HROWS, :] = turned[:, :CORR].astype(jnp.bfloat16)
            hankel[s, c, HROWS:, :] = jnp.zeros((LANES - HROWS, CORR), jnp.bfloat16)
            return carry

        lax.fori_loop(0, CH, one, 0, unroll=3)

    @pl.loop(0, 3)
    def _(s):
        lags(s)

    lane = lax.broadcasted_iota(jnp.int32, (8, LANES), 1)
    live = lane < TLEN
    flip = (HROWS - 1 - lane) & (LANES - 1)
    owner = blocks[y] // 2
    owner_y, owner_z = owner // 8, (owner // 2) % 4
    gathers = []
    for i, (a, b) in enumerate(CHUNKS):
        for k, copy in sends:
            if k == i:
                copy.wait_recv()
        here = jnp.logical_and(owner_y == y, owner_z == z)

        def kept(c):
            return jnp.where(
                here, cand[i][y, z, c].astype(jnp.float32), pieces[i][owner_y, owner_z, c].astype(jnp.float32)
            )

        def one(c, carry):
            v = kept(c)
            v = jnp.where(live, v, 0.0)
            mean = jnp.sum(v, axis=1, keepdims=True) * (1.0 / TLEN)
            dev = jnp.where(live, v - mean, 0.0)
            spread = jnp.sqrt(jnp.sum(dev * dev, axis=1, keepdims=True) * (1.0 / TLEN) + EPS)
            u = dev / (spread * TLEN)
            got[i][z, c] = jnp.take_along_axis(u, flip, axis=1).astype(jnp.bfloat16)
            return carry

        lax.fori_loop(0, b - a, one, 0, unroll=5)
        for f in range(HELD[i] - (b - a)):
            got[i][z, b - a + f] = kept(b - a + f).astype(jnp.bfloat16)
        for d in range(1, 4):
            copy = remote(
                got[i].at[z], got[i].at[z], gather_send.at[i, d - 1], gather_recv.at[i, d - 1],
                at_tm(y, (z + d) % 4, h),
            )
            copy.start()
            gathers.append((i, copy))
        if i == 0:
            lags(3)

    def sum_copy(s, j):
        y2, h2 = s // 2, s % 2
        to_tm = y2 * 8 + z * 2 + h2
        to_sta = 4 * y + 2 * h + j
        itself = jnp.logical_and(to_tm == tm, to_sta == sta)
        src = part.at[s, pl.ds(16 * j, 16)]
        k = 2 * s + j
        return itself, src, remote(
            src, got_part.at[sta], part_send.at[k], part_recv.at[sta], {"tm": to_tm, "sta": to_sta}
        )

    wide_lane = lax.broadcasted_iota(jnp.int32, (ROWS, LANES), 1)
    for i, (a, b) in enumerate(CHUNKS):
        for k, copy in gathers:
            if k == i:
                copy.wait_recv()
        if i == 0:
            tables = []
            for f in range(2):
                table = jnp.transpose(got[0][:, b - a + f].astype(jnp.float32).reshape(ROWS, LANES))
                tables.append(jnp.where(h == 0, table[0:32], table[32:64]))
        for c in range(a, b):
            w = jnp.broadcast_to(tables[0][:, c : c + 1], (ROWS, LANES))
            u = got[i][:, c - a].astype(jnp.float32).reshape(ROWS, LANES)
            unit[c] = (u * w).astype(jnp.bfloat16)
            index[c] = wide_lane + jnp.broadcast_to(tables[1][:, c : c + 1], (ROWS, LANES)).astype(jnp.int32)

        @pl.loop(0, 4)
        def _(s):
            if i == 0:
                acc = [jnp.zeros((ROWS, LANES), jnp.float32) for _ in range(4)]
            else:
                acc = [part[s, :, LANES * m : LANES * (m + 1)] for m in range(4)]
            for c in range(a, b):
                corr = jnp.dot(unit[c], hankel[s, c], preferred_element_type=jnp.float32)
                corr = corr * scale[s, pl.ds(c, 1), :]
                where = index[c]
                inside = where < LANES
                at = where & (LANES - 1)
                turned = [
                    jnp.take_along_axis(corr[:, LANES * m : LANES * (m + 1)], at, axis=1) for m in range(5)
                ]
                acc = [v + jnp.where(inside, turned[m], turned[m + 1]) for m, v in enumerate(acc)]
            for m in range(4):
                part[s, :, LANES * m : LANES * (m + 1)] = acc[m]
            if i == len(CHUNKS) - 1:
                for j in range(2):
                    itself, src, away = sum_copy(s, j)

                    @pl.when(jnp.logical_not(itself))
                    def _():
                        away.start()

                    @pl.when(itself)
                    def _():
                        got_part[sta] = src[...]

    for s in range(8):
        @pl.when(jnp.logical_not(jnp.logical_and(mine, sta == s)))
        def _():
            remote(
                part.at[0, pl.ds(0, 16)], got_part.at[s], part_send.at[0], part_recv.at[s],
                {"tm": source_tm, "sta": s},
            ).wait_recv()

    total = got_part[0]
    for s in range(1, 8):
        total = total + got_part[s]
    out[...] = total
    @pl.when(h == 0)
    def _():
        for k in range(4):
            halo_copy(k).wait_send()

    for _, copy in sends + gathers:
        copy.wait_send()
    for s in range(4):
        for j in range(2):
            itself, _, away = sum_copy(s, j)

            @pl.when(jnp.logical_not(itself))
            def _():
                away.wait_send()


ANY = pl.BlockSpec(memory_space=pl.ANY)
IN_VMEM = pl.BlockSpec(memory_space=VMEM)
IN_SMEM = pl.BlockSpec(memory_space=pltpu.SMEM)


def shards(waveforms, templates, available, moveout, bank_blocks):
    bf16, f32, i32 = jnp.bfloat16, jnp.float32, jnp.int32
    return pl.pallas_call(
        kernel,
        out_shape=jax.ShapeDtypeStruct((16, SEG), f32),
        in_specs=[IN_SMEM, ANY, ANY, ANY, ANY],
        out_specs=IN_VMEM,
        scratch_shapes=[
            *(VMEM((2, 2, b - a, 32, TLEN), bf16) for a, b in CHUNKS),
            VMEM((2, 2, CH, 2, 64), i32),
            *(VMEM((2, 4, n, 8, LANES), bf16) for n in HELD),
            *(VMEM((2, 4, n, 8, LANES), bf16) for n in HELD),
            *(VMEM((4, n, 8, LANES), bf16) for n in HELD),
            VMEM((2, 2, CH, SEG), bf16),
            VMEM((2, CH, 256), bf16),
            VMEM((4, ROWS, EXT), f32),
            VMEM((4, ROWS, CORR), f32),
            VMEM((4, CH, LANES, CORR), bf16),
            VMEM((CH, ROWS, LANES), bf16),
            VMEM((CH, ROWS, LANES), i32),
            VMEM((4, ROWS, SEG), f32),
            VMEM((8, 16, SEG), f32),
            DMA((5,)), DMA((3,)), DMA((3,)), DMA((4,)), DMA((2,)), DMA((4,)), DMA((4,)),
            DMA((2, 7)), DMA((2, 7)), DMA((2, 3)), DMA((2, 3)), DMA((8,)), DMA((8,)),
        ],
        compiler_params=pltpu.CompilerParams(collective_id=1, has_side_effects=True, vmem_limit_bytes=60 * MIB),
    )(
        bank_blocks,
        jnp.transpose(templates, (0, 2, 1, 3)),
        jnp.transpose(available, (2, 0, 1)),
        jnp.transpose(moveout, (2, 0, 1)),
        waveforms,
    )


def solution(mesh):
    in_specs = (
        P("sta", "tm"),
        P("tm", None, "sta", None),
        P("tm", None, "sta"),
        P("tm", None, "sta"),
        P(),
    )
    return jax.shard_map(shards, mesh=mesh, in_specs=in_specs, out_specs=P("sta", "tm"), check_vma=False)
```

time: 326 us -> 42.4 us (0.13)
  the two profiles are of different devices: /device:TPU:0 before, /device:TPU:17 now
where the time goes in v2:
time: 42.4 us; the launch traced here: 42.2 us
  Pallas kernels  40.8 us (96%)
  local copies, waits for them, and re-layouts  1.38 us (3%)
    pallas_call x1, Pallas kernels, shards(): pl.pallas_call(kernel, out_shape=jax.ShapeDtypeStruct((16, SEG), f32), in...  40.8 us
    unnamed x1, local copies, waits for them, and re-layouts  1.38 us

profile of v2, /device:TPU:17, one launch (start us, length us, event | category | flops | bytes accessed | tf_op | source)
XLA Modules:
  0.0 42.2 jit_solution(8298947501028835629)
XLA Ops:
  0.0 40.8 %shard_map.55 = f32[16,512]{1,0:T(8,128)} custom-call(s32[2]{0:T(128)} %blocks.1, bf16[2,30,64,100]{3,2,1,0:T(8,128)(2,1)} %bitcast.3, s32[30,2,64]{2,1,0:T(2,128)} %bitcast.4, s32[30,2,64]{2,1,0:T(2,128)} %bitcast.5, bf16[30,512]{1,0:T(8,128)(2,1)} %wave.1), custom_call_target="tpu_custom_call" | custom-call | tf_op jit(solution)/shard_map/pallas_call | solution.py:323
  40.9 1.4 %copy.7 = f32[16,512]{1,0:T(8,128)} copy(f32[16,512]{1,0:T(8,128)} %shard_map.55) | data formatting | bytes 65536

commit v3 on v2

v3 whole, which is shorter than its diff:
```python
import jax
import jax.numpy as jnp
from jax import lax
from jax.experimental import pallas as pl
from jax.experimental.pallas import tpu as pltpu
from jax.sharding import PartitionSpec as P

TLEN = 100
EPS = 1e-06
SEG = 512
RUN = 1024
EXT = 1280
CORR = 1152
CH = 30
ROWS = 64
LANES = 128
HROWS = 112
CHUNKS = ((0, 15), (15, 30))
HELD = tuple(b - a + (2 if a == 0 else 0) for a, b in CHUNKS)
N = len(CHUNKS)
MESH = pl.DeviceIdType.MESH
VMEM = pltpu.VMEM
DMA = pltpu.SemaphoreType.DMA
MIB = 1 << 20


def place():
    tm = lax.axis_index("tm")
    return tm // 8, (tm // 2) % 4, tm % 2


def at_tm(y, z, h):
    return {"tm": y * 8 + z * 2 + h}


def remote(src, dst, send, recv, device):
    return pltpu.make_async_remote_copy(
        src_ref=src, dst_ref=dst, send_sem=send, recv_sem=recv, device_id=device, device_id_type=MESH
    )


def left(x, n):
    return pltpu.roll(x, x.shape[1] - n, 1)


def window_sum(x):
    two = x + left(x, 1)
    four = two + left(two, 2)
    eight = four + left(four, 4)
    sixteen = eight + left(eight, 8)
    half = sixteen + left(sixteen, 16)
    full = half + left(half, 32)
    return full + left(half, 64) + left(four, 96)


def kernel(blocks, bank, avail, shift, wave, out, *scratch):
    cores, cand, pieces, got = (scratch[k * N : k * N + N] for k in range(4))
    (
        core_flags, got_wave, got_halo, ext, scale, hankel, unit, index, part, got_part,
        local_sem, wave_send, wave_recv, halo_send, halo_recv, core_send, core_recv,
        piece_send, piece_recv, gather_send, gather_recv, part_send, part_recv,
    ) = scratch[4 * N :]
    y, z, h = place()
    tm = lax.axis_index("tm")
    sta = lax.axis_index("sta")
    flags = (avail, shift)
    locals_ = [
        pltpu.make_async_copy(bank.at[:, a:b, pl.ds(32 * h, 32)], cores[i].at[h], local_sem.at[i])
        for i, (a, b) in enumerate(CHUNKS)
    ]
    local_flags = [pltpu.make_async_copy(flags[f], core_flags.at[h, f], local_sem.at[N + f]) for f in range(2)]
    local_wave = pltpu.make_async_copy(wave, got_wave.at[h], local_sem.at[N + 2])
    for copy in local_flags + locals_ + [local_wave]:
        copy.start()

    source_h = (sta // 2) % 2
    mine = source_h == h
    source_tm = y * 8 + z * 2 + source_h
    barrier = pltpu.get_barrier_semaphore()
    for d in range(1, 16):
        pl.semaphore_signal(barrier, inc=1, device_id={"tm": (tm + d) % 16}, device_id_type=MESH)
    for s in range(8):
        @pl.when(jnp.logical_not(jnp.logical_and(mine, sta == s)))
        def _():
            pl.semaphore_signal(barrier, inc=1, device_id={"tm": source_tm, "sta": s}, device_id_type=MESH)

    @pl.when(mine)
    def _():
        pl.semaphore_wait(barrier, 22)

    @pl.when(jnp.logical_not(mine))
    def _():
        pl.semaphore_wait(barrier, 23)

    partner = at_tm(y, z, 1 - h)
    to_flags = [
        remote(flags[f], core_flags.at[h, f], core_send.at[N + f], core_recv.at[N + f], partner) for f in range(2)
    ]
    to_core = [
        remote(
            bank.at[:, a:b, pl.ds(32 * (1 - h), 32)], cores[i].at[h], core_send.at[i], core_recv.at[i], partner
        )
        for i, (a, b) in enumerate(CHUNKS)
    ]
    to_wave = remote(wave, got_wave.at[h], wave_send, wave_recv, partner)
    before_y, before_z = jnp.where(z > 0, y, 1 - y), (z + 3) % 4

    def halo_copy(k):
        return remote(wave.at[:, pl.ds(0, 256)], got_halo, halo_send.at[k], halo_recv, at_tm(before_y, before_z, k))

    for copy in to_flags + to_core[:1]:
        copy.start()

    @pl.when(h == 0)
    def _():
        for k in range(2):
            halo_copy(k).start()

    for copy in to_core[1:] + [to_wave]:
        copy.start()

    for copy in local_flags + to_flags:
        copy.wait()
    sends = []
    for i, (a, b) in enumerate(CHUNKS):
        locals_[i].wait()
        to_core[i].wait()
        for q in range(2):
            block = blocks[q]
            core, slot = (block // 2) % 2, block % 2
            for z2 in range(4):
                cand[i][q, z2, 0 : b - a, :, 0:TLEN] = cores[i][core, slot, :, 8 * z2 : 8 * z2 + 8]
            if i == 0:
                for f in range(2):
                    both = core_flags[core, f].astype(jnp.float32)
                    rows = jnp.where(slot == 0, both[:, 0, :], both[:, 1, :]).astype(jnp.bfloat16)
                    for z2 in range(4):
                        top = min(8, CH - 8 * z2)
                        cand[i][q, z2, b - a + f, 0:top, 0:64] = rows[8 * z2 : 8 * z2 + top]
        for d in range(1, 8):
            y2, z2 = (y + d // 4) % 2, (z + d) % 4
            copy = remote(
                cand[i].at[y2, z2], pieces[i].at[y, z], piece_send.at[i, d - 1], piece_recv.at[i, d - 1],
                at_tm(y2, z2, h),
            )
            copy.start()
            sends.append((i, copy))

    local_wave.wait()
    to_wave.wait()
    remote(wave.at[:, pl.ds(0, 256)], got_halo, halo_send.at[0], halo_recv, partner).wait_recv()
    for core in range(2):
        ext[0:CH, SEG * core : SEG * core + SEG] = got_wave[core].astype(jnp.float32)
    tail = got_halo[...].astype(jnp.float32)
    ext[0:CH, RUN:EXT] = jnp.where(jnp.logical_and(y == 1, z == 3), jnp.zeros_like(tail), tail)

    def lags(c, carry):
        wide = jnp.broadcast_to(ext[pl.ds(c, 1), :], (HROWS, EXT))
        turned = pltpu.roll(wide, EXT - (HROWS - 1), 1, stride=1, stride_axis=0)
        hankel[c] = turned[:, :CORR].astype(jnp.bfloat16)
        return carry

    lax.fori_loop(0, CH, lags, 0, unroll=5)
    x = ext[...]
    first = window_sum(x)[:, :CORR] * (1.0 / TLEN)
    second = window_sum(x * x)[:, :CORR] * (1.0 / TLEN)
    scale[...] = lax.rsqrt(second - first * first + EPS)

    lane = lax.broadcasted_iota(jnp.int32, (8, LANES), 1)
    live = lane < TLEN
    flip = (HROWS - 1 - lane) & (LANES - 1)
    owner = blocks[y] // 2
    owner_y, owner_z = owner // 8, (owner // 2) % 4
    here = jnp.logical_and(owner_y == y, owner_z == z)
    own = 4 * y + z
    gathers = []
    for i, (a, b) in enumerate(CHUNKS):
        for k, copy in sends:
            if k == i:
                copy.wait_recv()

        def kept(c):
            return jnp.where(
                here, cand[i][y, z, c].astype(jnp.float32), pieces[i][owner_y, owner_z, c].astype(jnp.float32)
            )

        for c in range(b - a):
            v = jnp.where(live, kept(c), 0.0)
            mean = jnp.sum(v, axis=1, keepdims=True) * (1.0 / TLEN)
            dev = jnp.where(live, v - mean, 0.0)
            spread = jnp.sqrt(jnp.sum(dev * dev, axis=1, keepdims=True) * (1.0 / TLEN) + EPS)
            u = dev / (spread * TLEN)
            got[i][own, c] = jnp.take_along_axis(u, flip, axis=1).astype(jnp.bfloat16)
        for c in range(b - a, HELD[i]):
            got[i][own, c] = kept(c).astype(jnp.bfloat16)
        for d in range(1, 8):
            copy = remote(
                got[i].at[own], got[i].at[own], gather_send.at[i, d - 1], gather_recv.at[i, d - 1],
                at_tm((y + d // 4) % 2, (z + d) % 4, h),
            )
            copy.start()
            gathers.append((i, copy))

    def sum_copy(r, h2):
        to_tm = y * 8 + z * 2 + h2
        to_sta = 4 * (r // 2) + 2 * h + r % 2
        itself = jnp.logical_and(h == h2, to_sta == sta)
        src = part.at[pl.ds(16 * r, 16), pl.ds(SEG * h2, SEG)]
        return itself, src, remote(
            src, got_part.at[sta], part_send.at[2 * r + h2], part_recv.at[sta], {"tm": to_tm, "sta": to_sta}
        )

    wide_lane = lax.broadcasted_iota(jnp.int32, (ROWS, LANES), 1)
    for i, (a, b) in enumerate(CHUNKS):
        for k, copy in gathers:
            if k == i:
                copy.wait_recv()
        if i == 0:
            tables = []
            for f in range(2):
                halves = []
                for q in range(2):
                    table = jnp.transpose(
                        got[0][4 * q : 4 * q + 4, b - a + f].astype(jnp.float32).reshape(32, LANES)
                    )
                    halves.append(jnp.where(h == 0, table[0:32], table[32:64]))
                tables.append(jnp.concatenate(halves, axis=0))
        for c in range(a, b):
            w = jnp.broadcast_to(tables[0][:, c : c + 1], (ROWS, LANES))
            u = got[i][:, c - a].astype(jnp.float32).reshape(ROWS, LANES)
            unit[c] = (u * w).astype(jnp.bfloat16)
            index[c] = wide_lane + jnp.broadcast_to(tables[1][:, c : c + 1], (ROWS, LANES)).astype(jnp.int32)
        if i == N - 1:
            for _, copy in sends:
                copy.wait_send()

            @pl.when(h == 0)
            def _():
                for k in range(2):
                    halo_copy(k).wait_send()

        @pl.loop(0, 4)
        def _(r):
            rows = pl.ds(pl.multiple_of(16 * r, 16), 16)
            if i == 0:
                acc = [jnp.zeros((16, LANES), jnp.float32) for _ in range(8)]
            else:
                acc = [part[rows, LANES * m : LANES * (m + 1)] for m in range(8)]
            for c in range(a, b):
                corr = jnp.dot(unit[c, rows, 0:HROWS], hankel[c], preferred_element_type=jnp.float32)
                corr = corr * scale[pl.ds(c, 1), :]
                where = index[c, rows, :]
                inside = where < LANES
                at = where & (LANES - 1)
                turned = [
                    jnp.take_along_axis(corr[:, LANES * m : LANES * (m + 1)], at, axis=1) for m in range(9)
                ]
                acc = [v + jnp.where(inside, turned[m], turned[m + 1]) for m, v in enumerate(acc)]
            for m in range(8):
                part[rows, LANES * m : LANES * (m + 1)] = acc[m]
            if i == N - 1:
                for h2 in range(2):
                    itself, src, away = sum_copy(r, h2)

                    @pl.when(jnp.logical_not(itself))
                    def _():
                        away.start()

                    @pl.when(itself)
                    def _():
                        got_part[sta] = src[...]

    for _, copy in gathers:
        copy.wait_send()
    for s in range(8):
        @pl.when(jnp.logical_not(jnp.logical_and(mine, sta == s)))
        def _():
            remote(
                part.at[pl.ds(0, 16), pl.ds(0, SEG)], got_part.at[s], part_send.at[0], part_recv.at[s],
                {"tm": source_tm, "sta": s},
            ).wait_recv()

    total = got_part[0]
    for s in range(1, 8):
        total = total + got_part[s]
    out[...] = total
    for r in range(4):
        for h2 in range(2):
            itself, _, away = sum_copy(r, h2)

            @pl.when(jnp.logical_not(itself))
            def _():
                away.wait_send()


ANY = pl.BlockSpec(memory_space=pl.ANY)
IN_VMEM = pl.BlockSpec(memory_space=VMEM)
IN_SMEM = pl.BlockSpec(memory_space=pltpu.SMEM)


def shards(waveforms, templates, available, moveout, bank_blocks):
    bf16, f32, i32 = jnp.bfloat16, jnp.float32, jnp.int32
    return pl.pallas_call(
        kernel,
        out_shape=jax.ShapeDtypeStruct((16, SEG), f32),
        in_specs=[IN_SMEM, ANY, ANY, ANY, ANY],
        out_specs=IN_VMEM,
        scratch_shapes=[
            *(VMEM((2, 2, b - a, 32, TLEN), bf16) for a, b in CHUNKS),
            *(VMEM((2, 4, n, 8, LANES), bf16) for n in HELD),
            *(VMEM((2, 4, n, 8, LANES), bf16) for n in HELD),
            *(VMEM((8, n, 8, LANES), bf16) for n in HELD),
            VMEM((2, 2, CH, 2, 64), i32),
            VMEM((2, CH, SEG), bf16),
            VMEM((CH, 256), bf16),
            VMEM((32, EXT), f32),
            VMEM((32, CORR), f32),
            VMEM((CH, HROWS, CORR), bf16),
            VMEM((CH, ROWS, LANES), bf16),
            VMEM((CH, ROWS, LANES), i32),
            VMEM((ROWS, RUN), f32),
            VMEM((8, 16, SEG), f32),
            DMA((N + 3,)), DMA, DMA, DMA((2,)), DMA, DMA((N + 2,)), DMA((N + 2,)),
            DMA((N, 7)), DMA((N, 7)), DMA((N, 7)), DMA((N, 7)), DMA((8,)), DMA((8,)),
        ],
        compiler_params=pltpu.CompilerParams(collective_id=1, has_side_effects=True, vmem_limit_bytes=60 * MIB),
    )(
        bank_blocks,
        jnp.transpose(templates, (0, 2, 1, 3)),
        jnp.transpose(available, (2, 0, 1)),
        jnp.transpose(moveout, (2, 0, 1)),
        waveforms,
    )


def solution(mesh):
    in_specs = (
        P("sta", "tm"),
        P("tm", None, "sta", None),
        P("tm", None, "sta"),
        P("tm", None, "sta"),
        P(),
    )
    return jax.shard_map(shards, mesh=mesh, in_specs=in_specs, out_specs=P("sta", "tm"), check_vma=False)
```

time: 42.4 us -> 37.1 us (0.88)
  the two profiles are of different devices: /device:TPU:17 before, /device:TPU:11 now
where the time goes in v3:
time: 37.1 us; the launch traced here: 36.9 us
  Pallas kernels  35.5 us (96%)
  local copies, waits for them, and re-layouts  1.38 us (4%)
    pallas_call x1, Pallas kernels, shards(): pl.pallas_call(kernel, out_shape=jax.ShapeDtypeStruct((16, SEG), f32), in...  35.5 us
    unnamed x1, local copies, waits for them, and re-layouts  1.38 us

profile of v3, /device:TPU:11, one launch (start us, length us, event | category | flops | bytes accessed | tf_op | source)
XLA Modules:
  0.0 36.9 jit_solution(1856468299394226312)
XLA Ops:
  0.0 35.5 %shard_map.55 = f32[16,512]{1,0:T(8,128)} custom-call(s32[2]{0:T(128)} %blocks.1, bf16[2,30,64,100]{3,2,1,0:T(8,128)(2,1)} %bitcast.3, s32[30,2,64]{2,1,0:T(2,128)} %bitcast.4, s32[30,2,64]{2,1,0:T(2,128)} %bitcast.5, bf16[30,512]{1,0:T(8,128)(2,1)} %wave.1), custom_call_target="tpu_custom_call" | custom-call | tf_op jit(solution)/shard_map/pallas_call | solution.py:303
  35.5 1.4 %copy.7 = f32[16,512]{1,0:T(8,128)} copy(f32[16,512]{1,0:T(8,128)} %shard_map.55) | data formatting | bytes 65536

commit v4 on v3

--- a/solution.py
+++ b/solution.py
@@ -53,10 +53,10 @@
     return full + left(half, 64) + left(four, 96)
 
 
-def kernel(blocks, bank, avail, shift, wave, out, *scratch):
+def kernel(which, bank, avail, shift, wave, out, *scratch):
     cores, cand, pieces, got = (scratch[k * N : k * N + N] for k in range(4))
     (
-        core_flags, got_wave, got_halo, ext, scale, hankel, unit, index, part, got_part,
+        blocks, core_flags, got_wave, got_halo, ext, scale, hankel, unit, index, part, got_part,
         local_sem, wave_send, wave_recv, halo_send, halo_recv, core_send, core_recv,
         piece_send, piece_recv, gather_send, gather_recv, part_send, part_recv,
     ) = scratch[4 * N :]
@@ -70,29 +70,35 @@
     ]
     local_flags = [pltpu.make_async_copy(flags[f], core_flags.at[h, f], local_sem.at[N + f]) for f in range(2)]
     local_wave = pltpu.make_async_copy(wave, got_wave.at[h], local_sem.at[N + 2])
-    for copy in local_flags + locals_ + [local_wave]:
+    local_blocks = pltpu.make_async_copy(which, blocks, local_sem.at[N + 3])
+    for copy in [local_blocks] + local_flags + locals_ + [local_wave]:
         copy.start()
 
     source_h = (sta // 2) % 2
     mine = source_h == h
     source_tm = y * 8 + z * 2 + source_h
     barrier = pltpu.get_barrier_semaphore()
-    for d in range(1, 16):
-        pl.semaphore_signal(barrier, inc=1, device_id={"tm": (tm + d) % 16}, device_id_type=MESH)
+    partner = at_tm(y, z, 1 - h)
+    for d in range(1, 8):
+        pl.semaphore_signal(barrier, inc=1, device_id=at_tm((y + d // 4) % 2, (z + d) % 4, h), device_id_type=MESH)
+    pl.semaphore_signal(barrier, inc=1, device_id=partner, device_id_type=MESH)
+    after = at_tm(jnp.where(z < 3, y, 1 - y), (z + 1) % 4, 0)
+
+    @pl.when(h == 1)
+    def _():
+        pl.semaphore_signal(barrier, inc=1, device_id=after, device_id_type=MESH)
+
     for s in range(8):
         @pl.when(jnp.logical_not(jnp.logical_and(mine, sta == s)))
         def _():
             pl.semaphore_signal(barrier, inc=1, device_id={"tm": source_tm, "sta": s}, device_id_type=MESH)
 
-    @pl.when(mine)
-    def _():
-        pl.semaphore_wait(barrier, 22)
-
-    @pl.when(jnp.logical_not(mine))
-    def _():
-        pl.semaphore_wait(barrier, 23)
-
-    partner = at_tm(y, z, 1 - h)
+    for first in range(2):
+        for both in range(2):
+            @pl.when(jnp.logical_and(h == first, mine if both else jnp.logical_not(mine)))
+            def _():
+                pl.semaphore_wait(barrier, 17 - first - both)
+
     to_flags = [
         remote(flags[f], core_flags.at[h, f], core_send.at[N + f], core_recv.at[N + f], partner) for f in range(2)
     ]
@@ -119,7 +125,7 @@
     for copy in to_core[1:] + [to_wave]:
         copy.start()
 
-    for copy in local_flags + to_flags:
+    for copy in [local_blocks] + local_flags + to_flags:
         copy.wait()
     sends = []
     for i, (a, b) in enumerate(CHUNKS):
@@ -293,9 +299,8 @@
                 away.wait_send()
 
 
-ANY = pl.BlockSpec(memory_space=pl.ANY)
+ANY = pl.BlockSpec(memory_space=pltpu.HBM)
 IN_VMEM = pl.BlockSpec(memory_space=VMEM)
-IN_SMEM = pl.BlockSpec(memory_space=pltpu.SMEM)
 
 
 def shards(waveforms, templates, available, moveout, bank_blocks):
@@ -303,13 +308,14 @@
     return pl.pallas_call(
         kernel,
         out_shape=jax.ShapeDtypeStruct((16, SEG), f32),
-        in_specs=[IN_SMEM, ANY, ANY, ANY, ANY],
+        in_specs=[ANY, ANY, ANY, ANY, ANY],
         out_specs=IN_VMEM,
         scratch_shapes=[
             *(VMEM((2, 2, b - a, 32, TLEN), bf16) for a, b in CHUNKS),
             *(VMEM((2, 4, n, 8, LANES), bf16) for n in HELD),
             *(VMEM((2, 4, n, 8, LANES), bf16) for n in HELD),
             *(VMEM((8, n, 8, LANES), bf16) for n in HELD),
+            pltpu.SMEM((2,), i32),
             VMEM((2, 2, CH, 2, 64), i32),
             VMEM((2, CH, SEG), bf16),
             VMEM((CH, 256), bf16),
@@ -320,16 +326,16 @@
             VMEM((CH, ROWS, LANES), i32),
             VMEM((ROWS, RUN), f32),
             VMEM((8, 16, SEG), f32),
-            DMA((N + 3,)), DMA, DMA, DMA((2,)), DMA, DMA((N + 2,)), DMA((N + 2,)),
+            DMA((N + 4,)), DMA, DMA, DMA((2,)), DMA, DMA((N + 2,)), DMA((N + 2,)),
             DMA((N, 7)), DMA((N, 7)), DMA((N, 7)), DMA((N, 7)), DMA((8,)), DMA((8,)),
         ],
-        compiler_params=pltpu.CompilerParams(collective_id=1, has_side_effects=True, vmem_limit_bytes=60 * MIB),
+        compiler_params=pltpu.CompilerParams(collective_id=1, has_side_effects=True, vmem_limit_bytes=32 * MIB),
     )(
-        bank_blocks,
-        jnp.transpose(templates, (0, 2, 1, 3)),
-        jnp.transpose(available, (2, 0, 1)),
-        jnp.transpose(moveout, (2, 0, 1)),
-        waveforms,
+        pltpu.with_memory_space_constraint(bank_blocks, pltpu.HBM),
+        pltpu.with_memory_space_constraint(jnp.transpose(templates, (0, 2, 1, 3)), pltpu.HBM),
+        pltpu.with_memory_space_constraint(jnp.transpose(available, (2, 0, 1)), pltpu.HBM),
+        pltpu.with_memory_space_constraint(jnp.transpose(moveout, (2, 0, 1)), pltpu.HBM),
+        pltpu.with_memory_space_constraint(waveforms, pltpu.HBM),
     )
 
 

time: 37.1 us -> 34.8 us (0.938)
  Pallas kernels: 35.5 us -> 34.1 us
  local copies, waits for them, and re-layouts: 1.38 us -> 0.62 us
    pallas_call x1, Pallas kernels: 35.5 us -> 34.1 us  [shards(): pl.pallas_call(kernel, out_shape=jax.ShapeDtypeStruct((16, SEG), f32), in...]
    unnamed x1, local copies, waits for them, and re-layouts: 1.38 us -> 0.62 us
where the time goes in v4:
time: 34.8 us; the launch traced here: 34.7 us
  Pallas kernels  34.1 us (98%)
  local copies, waits for them, and re-layouts  0.62 us (2%)
    pallas_call x1, Pallas kernels, shards(): pl.pallas_call(kernel, out_shape=jax.ShapeDtypeStruct((16, SEG), f32), in...  34.1 us

profile of v4, /device:TPU:11, one launch (start us, length us, event | category | flops | bytes accessed | tf_op | source)
XLA Modules:
  0.0 34.7 jit_solution(8083662858145104362)
XLA Ops:
  0.0 34.1 %shard_map.55 = f32[16,512]{1,0:T(8,128)S(1)} custom-call(s32[2]{0:T(128)} %which.1, bf16[2,30,64,100]{3,2,1,0:T(8,128)(2,1)} %bitcast.3, s32[30,2,64]{2,1,0:T(2,128)} %bitcast.4, s32[30,2,64]{2,1,0:T(2,128)} %bitcast.5, bf16[30,512]{1,0:T(8,128)(2,1)} %wave.1), custom_call_target="tpu_custom_call" | custom-call | tf_op jit(solution)/shard_map/pallas_call | solution.py:308
  34.1 0.6 %copy.7 = f32[16,512]{1,0:T(8,128)} copy(f32[16,512]{1,0:T(8,128)S(1)} %shard_map.55) | data formatting | bytes 65536

commit v5 on v4

--- a/solution.py
+++ b/solution.py
@@ -16,8 +16,10 @@
 LANES = 128
 HROWS = 112
 CHUNKS = ((0, 15), (15, 30))
-HELD = tuple(b - a + (2 if a == 0 else 0) for a, b in CHUNKS)
 N = len(CHUNKS)
+HOSTS, GUESTS, QUARTER = 12, 3, 25
+HELD = (HOSTS + 1, HOSTS)
+FAR_FIRST = (6, 5, 7, 4, 2, 1, 3)
 MESH = pl.DeviceIdType.MESH
 VMEM = pltpu.VMEM
 DMA = pltpu.SemaphoreType.DMA
@@ -41,6 +43,13 @@
 
 def left(x, n):
     return pltpu.roll(x, x.shape[1] - n, 1)
+
+
+def guest(tiles, lane):
+    out = pltpu.roll(tiles[0], LANES - TLEN, 1)
+    for p in range(1, 4):
+        out = jnp.where(lane >= QUARTER * p, pltpu.roll(tiles[p], LANES - TLEN + QUARTER * p, 1), out)
+    return out
 
 
 def window_sum(x):
@@ -56,7 +65,7 @@
 def kernel(which, bank, avail, shift, wave, out, *scratch):
     cores, cand, pieces, got = (scratch[k * N : k * N + N] for k in range(4))
     (
-        blocks, core_flags, got_wave, got_halo, ext, scale, hankel, unit, index, part, got_part,
+        blocks, staging, late, core_flags, got_wave, got_halo, ext, scale, hankel, unit, index, part, got_part,
         local_sem, wave_send, wave_recv, halo_send, halo_recv, core_send, core_recv,
         piece_send, piece_recv, gather_send, gather_recv, part_send, part_recv,
     ) = scratch[4 * N :]
@@ -135,15 +144,24 @@
             block = blocks[q]
             core, slot = (block // 2) % 2, block % 2
             for z2 in range(4):
-                cand[i][q, z2, 0 : b - a, :, 0:TLEN] = cores[i][core, slot, :, 8 * z2 : 8 * z2 + 8]
+                cand[i][q, z2, 0:HOSTS, :, 0:TLEN] = cores[i][core, slot, 0:HOSTS, 8 * z2 : 8 * z2 + 8]
+            staging[q, :, :, 0:TLEN] = cores[i][core, slot, HOSTS:].astype(jnp.float32)
+            for k in range(HOSTS):
+                moved = pltpu.roll(staging[q, k // 4], TLEN - QUARTER * (k % 4), 1)
+                for z2 in range(4):
+                    cand[i][q, z2, k, :, TLEN : TLEN + QUARTER] = moved[
+                        8 * z2 : 8 * z2 + 8, TLEN : TLEN + QUARTER
+                    ].astype(jnp.bfloat16)
             if i == 0:
+                rows = []
                 for f in range(2):
                     both = core_flags[core, f].astype(jnp.float32)
-                    rows = jnp.where(slot == 0, both[:, 0, :], both[:, 1, :]).astype(jnp.bfloat16)
-                    for z2 in range(4):
-                        top = min(8, CH - 8 * z2)
-                        cand[i][q, z2, b - a + f, 0:top, 0:64] = rows[8 * z2 : 8 * z2 + top]
-        for d in range(1, 8):
+                    rows.append(jnp.where(slot == 0, both[:, 0, :], both[:, 1, :]))
+                rows = jnp.concatenate(rows, axis=1).astype(jnp.bfloat16)
+                for z2 in range(4):
+                    top = min(8, CH - 8 * z2)
+                    cand[i][q, z2, HOSTS, 0:top] = rows[8 * z2 : 8 * z2 + top]
+        for d in FAR_FIRST:
             y2, z2 = (y + d // 4) % 2, (z + d) % 4
             copy = remote(
                 cand[i].at[y2, z2], pieces[i].at[y, z], piece_send.at[i, d - 1], piece_recv.at[i, d - 1],
@@ -160,21 +178,19 @@
     tail = got_halo[...].astype(jnp.float32)
     ext[0:CH, RUN:EXT] = jnp.where(jnp.logical_and(y == 1, z == 3), jnp.zeros_like(tail), tail)
 
+    late[...] = pltpu.roll(ext[...], HROWS - TLEN, 1)
+
     def lags(c, carry):
-        wide = jnp.broadcast_to(ext[pl.ds(c, 1), :], (HROWS, EXT))
+        wide = jnp.broadcast_to(late[pl.ds(c, 1), :], (HROWS, EXT))
         turned = pltpu.roll(wide, EXT - (HROWS - 1), 1, stride=1, stride_axis=0)
         hankel[c] = turned[:, :CORR].astype(jnp.bfloat16)
         return carry
 
-    lax.fori_loop(0, CH, lags, 0, unroll=5)
-    x = ext[...]
-    first = window_sum(x)[:, :CORR] * (1.0 / TLEN)
-    second = window_sum(x * x)[:, :CORR] * (1.0 / TLEN)
-    scale[...] = lax.rsqrt(second - first * first + EPS)
+    lax.fori_loop(*CHUNKS[0], lags, 0, unroll=5)
 
     lane = lax.broadcasted_iota(jnp.int32, (8, LANES), 1)
     live = lane < TLEN
-    flip = (HROWS - 1 - lane) & (LANES - 1)
+    flip = (TLEN - 1 - lane) & (LANES - 1)
     owner = blocks[y] // 2
     owner_y, owner_z = owner // 8, (owner // 2) % 4
     here = jnp.logical_and(owner_y == y, owner_z == z)
@@ -190,22 +206,34 @@
                 here, cand[i][y, z, c].astype(jnp.float32), pieces[i][owner_y, owner_z, c].astype(jnp.float32)
             )
 
-        for c in range(b - a):
-            v = jnp.where(live, kept(c), 0.0)
+        tiles = [kept(k) for k in range(HOSTS)]
+        units = []
+        for v in tiles + [guest(tiles[4 * g : 4 * g + 4], lane) for g in range(GUESTS)]:
+            v = jnp.where(live, v, 0.0)
             mean = jnp.sum(v, axis=1, keepdims=True) * (1.0 / TLEN)
             dev = jnp.where(live, v - mean, 0.0)
             spread = jnp.sqrt(jnp.sum(dev * dev, axis=1, keepdims=True) * (1.0 / TLEN) + EPS)
             u = dev / (spread * TLEN)
-            got[i][own, c] = jnp.take_along_axis(u, flip, axis=1).astype(jnp.bfloat16)
-        for c in range(b - a, HELD[i]):
-            got[i][own, c] = kept(c).astype(jnp.bfloat16)
-        for d in range(1, 8):
+            units.append(jnp.take_along_axis(u, flip, axis=1))
+        for k in range(HOSTS):
+            moved = pltpu.roll(units[HOSTS + k // 4], TLEN - QUARTER * (k % 4), 1)
+            got[i][own, k] = jnp.where(live, units[k], moved).astype(jnp.bfloat16)
+        if i == 0:
+            got[i][own, HOSTS] = kept(HOSTS).astype(jnp.bfloat16)
+        for d in FAR_FIRST:
             copy = remote(
                 got[i].at[own], got[i].at[own], gather_send.at[i, d - 1], gather_recv.at[i, d - 1],
                 at_tm((y + d // 4) % 2, (z + d) % 4, h),
             )
             copy.start()
             gathers.append((i, copy))
+        if i == 0:
+            lax.fori_loop(*CHUNKS[1], lags, 0, unroll=5)
+
+    x = ext[...]
+    first = window_sum(x)[:, :CORR] * (1.0 / TLEN)
+    second = window_sum(x * x)[:, :CORR] * (1.0 / TLEN)
+    scale[...] = lax.rsqrt(second - first * first + EPS)
 
     def sum_copy(r, h2):
         to_tm = y * 8 + z * 2 + h2
@@ -222,19 +250,17 @@
             if k == i:
                 copy.wait_recv()
         if i == 0:
-            tables = []
-            for f in range(2):
-                halves = []
-                for q in range(2):
-                    table = jnp.transpose(
-                        got[0][4 * q : 4 * q + 4, b - a + f].astype(jnp.float32).reshape(32, LANES)
-                    )
-                    halves.append(jnp.where(h == 0, table[0:32], table[32:64]))
-                tables.append(jnp.concatenate(halves, axis=0))
+            halves = ([], [])
+            for q in range(2):
+                table = jnp.transpose(got[0][4 * q : 4 * q + 4, HOSTS].astype(jnp.float32).reshape(32, LANES))
+                for f in range(2):
+                    halves[f].append(jnp.where(h == 0, table[64 * f : 64 * f + 32], table[64 * f + 32 : 64 * f + 64]))
+            tables = [jnp.concatenate(half, axis=0) for half in halves]
+        tiles = [got[i][:, k].astype(jnp.float32).reshape(ROWS, LANES) for k in range(HOSTS)]
+        tiles = tiles + [guest(tiles[4 * g : 4 * g + 4], wide_lane) for g in range(GUESTS)]
         for c in range(a, b):
             w = jnp.broadcast_to(tables[0][:, c : c + 1], (ROWS, LANES))
-            u = got[i][:, c - a].astype(jnp.float32).reshape(ROWS, LANES)
-            unit[c] = (u * w).astype(jnp.bfloat16)
+            unit[c] = jnp.where(wide_lane < TLEN, tiles[c - a] * w, 0.0).astype(jnp.bfloat16)
             index[c] = wide_lane + jnp.broadcast_to(tables[1][:, c : c + 1], (ROWS, LANES)).astype(jnp.int32)
         if i == N - 1:
             for _, copy in sends:
@@ -316,6 +342,8 @@
             *(VMEM((2, 4, n, 8, LANES), bf16) for n in HELD),
             *(VMEM((8, n, 8, LANES), bf16) for n in HELD),
             pltpu.SMEM((2,), i32),
+            VMEM((2, GUESTS, 32, LANES), f32),
+            VMEM((32, EXT), f32),
             VMEM((2, 2, CH, 2, 64), i32),
             VMEM((2, CH, SEG), bf16),
             VMEM((CH, 256), bf16),

time: 34.8 us -> 33.4 us (0.960)
  Pallas kernels: 34.1 us -> 32.7 us
    pallas_call x1, Pallas kernels: 34.1 us -> 32.7 us  [shards(): pl.pallas_call(kernel, out_shape=jax.ShapeDtypeStruct((16, SEG), f32), in...]
where the time goes in v5:
time: 33.4 us; the launch traced here: 33.3 us
  Pallas kernels  32.7 us (98%)
  local copies, waits for them, and re-layouts  0.62 us (2%)
    pallas_call x1, Pallas kernels, shards(): pl.pallas_call(kernel, out_shape=jax.ShapeDtypeStruct((16, SEG), f32), in...  32.7 us

profile of v5, /device:TPU:11, one launch (start us, length us, event | category | flops | bytes accessed | tf_op | source)
XLA Modules:
  0.0 33.3 jit_solution(5799987134199356537)
XLA Ops:
  0.0 32.7 %shard_map.55 = f32[16,512]{1,0:T(8,128)S(1)} custom-call(s32[2]{0:T(128)} %which.1, bf16[2,30,64,100]{3,2,1,0:T(8,128)(2,1)} %bitcast.3, s32[30,2,64]{2,1,0:T(2,128)} %bitcast.4, s32[30,2,64]{2,1,0:T(2,128)} %bitcast.5, bf16[30,512]{1,0:T(8,128)(2,1)} %wave.1), custom_call_target="tpu_custom_call" | custom-call | tf_op jit(solution)/shard_map/pallas_call | solution.py:334
  32.7 0.6 %copy.7 = f32[16,512]{1,0:T(8,128)} copy(f32[16,512]{1,0:T(8,128)S(1)} %shard_map.55) | data formatting | bytes 65536

commit v6 on v5

--- a/solution.py
+++ b/solution.py
@@ -19,6 +19,7 @@
 N = len(CHUNKS)
 HOSTS, GUESTS, QUARTER = 12, 3, 25
 HELD = (HOSTS + 1, HOSTS)
+UNUSED = 512.0
 FAR_FIRST = (6, 5, 7, 4, 2, 1, 3)
 MESH = pl.DeviceIdType.MESH
 VMEM = pltpu.VMEM
@@ -255,22 +256,15 @@
                 table = jnp.transpose(got[0][4 * q : 4 * q + 4, HOSTS].astype(jnp.float32).reshape(32, LANES))
                 for f in range(2):
                     halves[f].append(jnp.where(h == 0, table[64 * f : 64 * f + 32], table[64 * f + 32 : 64 * f + 64]))
-            tables = [jnp.concatenate(half, axis=0) for half in halves]
+            used, moved = [jnp.concatenate(half, axis=0) for half in halves]
+            table = jnp.where(used > 0.5, moved, UNUSED)
         tiles = [got[i][:, k].astype(jnp.float32).reshape(ROWS, LANES) for k in range(HOSTS)]
         tiles = tiles + [guest(tiles[4 * g : 4 * g + 4], wide_lane) for g in range(GUESTS)]
         for c in range(a, b):
-            w = jnp.broadcast_to(tables[0][:, c : c + 1], (ROWS, LANES))
-            unit[c] = jnp.where(wide_lane < TLEN, tiles[c - a] * w, 0.0).astype(jnp.bfloat16)
-            index[c] = wide_lane + jnp.broadcast_to(tables[1][:, c : c + 1], (ROWS, LANES)).astype(jnp.int32)
-        if i == N - 1:
-            for _, copy in sends:
-                copy.wait_send()
-
-            @pl.when(h == 0)
-            def _():
-                for k in range(2):
-                    halo_copy(k).wait_send()
-
+            to = jnp.broadcast_to(table[:, c : c + 1], (ROWS, LANES))
+            keep = jnp.logical_and(wide_lane < TLEN, to < UNUSED)
+            unit[c] = jnp.where(keep, tiles[c - a], 0.0).astype(jnp.bfloat16)
+            index[c] = wide_lane + to.astype(jnp.int32)
         @pl.loop(0, 4)
         def _(r):
             rows = pl.ds(pl.multiple_of(16 * r, 16), 16)
@@ -302,8 +296,14 @@
                     def _():
                         got_part[sta] = src[...]
 
-    for _, copy in gathers:
+    for _, copy in sends + gathers:
         copy.wait_send()
+
+    @pl.when(h == 0)
+    def _():
+        for k in range(2):
+            halo_copy(k).wait_send()
+
     for s in range(8):
         @pl.when(jnp.logical_not(jnp.logical_and(mine, sta == s)))
         def _():

time: 33.4 us -> 33.3 us (level)
  no operation moved by 1% of the time
where the time goes in v6:
time: 33.3 us; the launch traced here: 33.2 us
  Pallas kernels  32.5 us (98%)
  local copies, waits for them, and re-layouts  0.62 us (2%)
    pallas_call x1, Pallas kernels, shards(): pl.pallas_call(kernel, out_shape=jax.ShapeDtypeStruct((16, SEG), f32), in...  32.5 us

profile of v6, /device:TPU:11, one launch (start us, length us, event | category | flops | bytes accessed | tf_op | source)
XLA Modules:
  0.0 33.2 jit_solution(5873147868946774050)
XLA Ops:
  0.0 32.5 %shard_map.55 = f32[16,512]{1,0:T(8,128)S(1)} custom-call(s32[2]{0:T(128)} %which.1, bf16[2,30,64,100]{3,2,1,0:T(8,128)(2,1)} %bitcast.3, s32[30,2,64]{2,1,0:T(2,128)} %bitcast.4, s32[30,2,64]{2,1,0:T(2,128)} %bitcast.5, bf16[30,512]{1,0:T(8,128)(2,1)} %wave.1), custom_call_target="tpu_custom_call" | custom-call | tf_op jit(solution)/shard_map/pallas_call | solution.py:334
  32.5 0.6 %copy.7 = f32[16,512]{1,0:T(8,128)} copy(f32[16,512]{1,0:T(8,128)S(1)} %shard_map.55) | data formatting | bytes 65536

commit v7 on v6

--- a/solution.py
+++ b/solution.py
@@ -141,7 +141,8 @@
     for i, (a, b) in enumerate(CHUNKS):
         locals_[i].wait()
         to_core[i].wait()
-        for q in range(2):
+        for away in (1, 0):
+            q = (y + away) % 2
             block = blocks[q]
             core, slot = (block // 2) % 2, block % 2
             for z2 in range(4):
@@ -162,14 +163,14 @@
                 for z2 in range(4):
                     top = min(8, CH - 8 * z2)
                     cand[i][q, z2, HOSTS, 0:top] = rows[8 * z2 : 8 * z2 + top]
-        for d in FAR_FIRST:
-            y2, z2 = (y + d // 4) % 2, (z + d) % 4
-            copy = remote(
-                cand[i].at[y2, z2], pieces[i].at[y, z], piece_send.at[i, d - 1], piece_recv.at[i, d - 1],
-                at_tm(y2, z2, h),
-            )
-            copy.start()
-            sends.append((i, copy))
+            for d in FAR_FIRST[:4] if away else FAR_FIRST[4:]:
+                z2 = (z + d) % 4
+                copy = remote(
+                    cand[i].at[q, z2], pieces[i].at[y, z], piece_send.at[i, d - 1], piece_recv.at[i, d - 1],
+                    at_tm(q, z2, h),
+                )
+                copy.start()
+                sends.append((i, copy))
 
     local_wave.wait()
     to_wave.wait()

time: 33.3 us -> 33.3 us (level)
  no operation moved by 1% of the time
where the time goes in v7:
time: 33.3 us; the launch traced here: 33.2 us
  Pallas kernels  32.6 us (98%)
  local copies, waits for them, and re-layouts  0.62 us (2%)
    pallas_call x1, Pallas kernels, shards(): pl.pallas_call(kernel, out_shape=jax.ShapeDtypeStruct((16, SEG), f32), in...  32.6 us

profile of v7, /device:TPU:11, one launch (start us, length us, event | category | flops | bytes accessed | tf_op | source)
XLA Modules:
  0.0 33.2 jit_solution(6579997269691975071)
XLA Ops:
  0.0 32.6 %shard_map.55 = f32[16,512]{1,0:T(8,128)S(1)} custom-call(s32[2]{0:T(128)} %which.1, bf16[2,30,64,100]{3,2,1,0:T(8,128)(2,1)} %bitcast.3, s32[30,2,64]{2,1,0:T(2,128)} %bitcast.4, s32[30,2,64]{2,1,0:T(2,128)} %bitcast.5, bf16[30,512]{1,0:T(8,128)(2,1)} %wave.1), custom_call_target="tpu_custom_call" | custom-call | tf_op jit(solution)/shard_map/pallas_call | solution.py:335
  32.6 0.6 %copy.7 = f32[16,512]{1,0:T(8,128)} copy(f32[16,512]{1,0:T(8,128)S(1)} %shard_map.55) | data formatting | bytes 65536
